TPU v7x, 256 devices: a whole 4x4x8 slice. The times are simulated.
256 devices in a mesh: tm: 64 (over x, z, core), feat: 4 (over y).
Axes of the slice: x: 4, y: 4, z: 8, core: 2. Of those that a mesh axis runs over, the one named last changes fastest.
Arguments:
- features: bfloat16 [131072, 512], P('tm'), may hold values from -64 to 64
- seg_lengths: int32 [128], replicated, may hold values from 1 to 4096, 131072 in all
Outputs:
- koopman: float32 [512, 512], P('feat')
- lag_error: float32 [128, 131072], P('feat', 'tm')
All inputs are finite; a program needn't handle non-finite values.
Results may differ from a plain program's by a relative error of at most 0.0037.
Values may be sent and summed in bfloat16 or wider, within the bound.
A program may use at most 64 MiB of HBM per device.

v0:
```python
import jax
import jax.numpy as jnp
from jax import lax
from jax.experimental import pallas as pl
from jax.experimental.pallas import tpu as pltpu
from jax.sharding import PartitionSpec as P

LAG = 64
NC = 128

RIDGE = 0.05
HIGHEST = lax.Precision.HIGHEST
LEAF = 128


def from_behind(shard, axis, by):
    count = lax.axis_size(axis)
    pairs = [(i, i + by) for i in range(count) if 0 <= i + by < count]
    return lax.ppermute(shard, axis, pairs)


def contract(left_rows, right_rows):
    return lax.dot_general(
        left_rows, right_rows, (((0,), (0,)), ((), ())), preferred_element_type=jnp.float32
    )


def exact_dot(left, right, left_dim=1, right_dim=0):
    return lax.dot_general(
        left,
        right,
        (((left_dim,), (right_dim,)), ((), ())),
        precision=HIGHEST,
        preferred_element_type=jnp.float32,
    )


def leaf_inverse(square):
    tiles = [square[8 * i : 8 * i + 8, :] for i in range(LEAF // 8)]
    lanes = lax.broadcasted_iota(jnp.int32, (8, LEAF), 1)
    subs = lax.broadcasted_iota(jnp.int32, (8, LEAF), 0)
    for j in range(LEAF - 1):
        own, sub = j // 8, j % 8
        row = jnp.broadcast_to(tiles[own][sub : sub + 1, :], (8, LEAF))
        pivot = jnp.broadcast_to(row[:, j : j + 1], (8, LEAF))
        at_pivot = lanes == j
        row = jnp.where(at_pivot, 1.0, row) / pivot
        for i in range(own, LEAF // 8):
            if i == own and sub == 7:
                continue
            factor = jnp.broadcast_to(tiles[i][:, j : j + 1], (8, LEAF))
            updated = jnp.where(at_pivot, 0.0, tiles[i]) - factor * row
            if i == own:
                updated = jnp.where(subs > sub, updated, tiles[i])
            tiles[i] = updated
    outs = []
    for i in range(LEAF // 8):
        rows = subs + 8 * i
        diag = jnp.sum(jnp.where(lanes == rows, tiles[i], 0.0), axis=1, keepdims=True)
        unit = jnp.where(lanes < rows, tiles[i], jnp.where(lanes == rows, 1.0, 0.0))
        outs.append(unit * lax.rsqrt(diag))
    return jnp.concatenate(outs, axis=0)


def whiten_kernel(
    index_ref, lengths_ref, moments_ref, sums_ref, koop_ref, first_ref, second_ref, offset_ref, work, cov
):
    feat_width = work.shape[0]
    blocks = feat_width // LEAF
    part = koop_ref.shape[0]
    pairs = jnp.maximum(lengths_ref[...] - LAG, 0).astype(jnp.float32)
    scale = 1.0 / (2.0 * jnp.sum(pairs, axis=1, keepdims=True))
    mean = sums_ref[0:1, :] * scale
    mean_cols = jnp.broadcast_to(mean, (LEAF, feat_width)).T
    rows_io = lax.broadcasted_iota(jnp.int32, (LEAF, LEAF), 0)
    lanes_io = lax.broadcasted_iota(jnp.int32, (LEAF, LEAF), 1)
    eye = rows_io == lanes_io
    trace = jnp.zeros((1, 1), jnp.float32)
    for k in range(blocks):
        square = moments_ref[2 * LEAF * k : 2 * LEAF * k + LEAF, LEAF * k : LEAF * k + LEAF]
        square = square * scale - mean_cols[LEAF * k : LEAF * k + LEAF, :] * mean[:, LEAF * k : LEAF * k + LEAF]
        diag = jnp.sum(jnp.where(eye, square, 0.0), axis=0, keepdims=True)
        trace = trace + jnp.sum(diag, axis=1, keepdims=True)
    ridge = RIDGE * (trace / feat_width)
    for k in range(blocks):
        for m in range(blocks):
            outer = mean_cols[LEAF * k : LEAF * k + LEAF, :] * mean[:, LEAF * m : LEAF * m + LEAF]
            block = moments_ref[2 * LEAF * k : 2 * LEAF * k + LEAF, LEAF * m : LEAF * m + LEAF] * scale - outer
            if k == m:
                block = block + jnp.where(eye, ridge, 0.0)
            work[LEAF * k : LEAF * k + LEAF, LEAF * m : LEAF * m + LEAF] = block
            straight = moments_ref[
                2 * LEAF * k + LEAF : 2 * LEAF * k + 2 * LEAF, LEAF * m : LEAF * m + LEAF
            ]
            turned = moments_ref[
                2 * LEAF * m + LEAF : 2 * LEAF * m + 2 * LEAF, LEAF * k : LEAF * k + LEAF
            ].T
            cov[LEAF * k : LEAF * k + LEAF, LEAF * m : LEAF * m + LEAF] = (straight + turned) * scale - outer

    def eliminate(k, carry):
        start = pl.multiple_of(k * LEAF, LEAF)
        inverse = leaf_inverse(work[pl.ds(start, LEAF), pl.ds(start, LEAF)])
        work[pl.ds(start, LEAF), pl.ds(start, LEAF)] = jnp.where(eye, 1.0, 0.0)
        panel = exact_dot(inverse, work[pl.ds(start, LEAF), :])
        wide_lanes = lax.broadcasted_iota(jnp.int32, (LEAF, feat_width), 1)
        below = jnp.where(wide_lanes >= start + LEAF, panel, 0.0)
        change = exact_dot(below, panel, 0, 0)
        in_block = (wide_lanes >= start) & (wide_lanes < start + LEAF)
        for i in range(blocks):
            old = work[LEAF * i : LEAF * i + LEAF, :]
            old = jnp.where(in_block & (k < i), 0.0, old)
            work[LEAF * i : LEAF * i + LEAF, :] = old - change[LEAF * i : LEAF * i + LEAF, :]
        work[pl.ds(start, LEAF), :] = panel
        return carry

    lax.fori_loop(0, blocks, eliminate, 0)
    rows_io = lax.broadcasted_iota(jnp.int32, (feat_width, feat_width), 0)
    lanes_io = lax.broadcasted_iota(jnp.int32, (feat_width, feat_width), 1)
    work[...] = jnp.where(rows_io >= lanes_io, work[...], 0.0)
    index = index_ref[0]
    comps = first_ref.shape[0]
    own_rows = work[pl.ds(pl.multiple_of(index * part, part), part), :]
    own_comps = work[pl.ds(pl.multiple_of(index * comps, comps), comps), :]
    stacked = jnp.concatenate([own_rows, own_comps], axis=0)
    koop = exact_dot(exact_dot(stacked, cov[...]), work[...], 1, 1)
    koop_ref[...] = koop[:part, :]
    first = own_comps.astype(jnp.bfloat16)
    second = exact_dot(koop[part:, :], work[...]).astype(jnp.bfloat16)
    first_ref[...] = first
    second_ref[...] = second
    gap = (first.astype(jnp.float32) - second.astype(jnp.float32)) * mean
    offset_ref[...] = jnp.broadcast_to(jnp.sum(gap, axis=1, keepdims=True), offset_ref.shape)


def whiten(index, lengths, moments, sums, part, comps):
    feat_width = moments.shape[1]
    vmem = pl.BlockSpec(memory_space=pltpu.VMEM)
    return pl.pallas_call(
        whiten_kernel,
        out_shape=(
            jax.ShapeDtypeStruct((part, feat_width), jnp.float32),
            jax.ShapeDtypeStruct((comps, feat_width), jnp.bfloat16),
            jax.ShapeDtypeStruct((comps, feat_width), jnp.bfloat16),
            jax.ShapeDtypeStruct((comps, 128), jnp.float32),
        ),
        in_specs=[pl.BlockSpec(memory_space=pltpu.SMEM), vmem, vmem, vmem],
        out_specs=(vmem, vmem, vmem, vmem),
        scratch_shapes=[
            pltpu.VMEM((feat_width, feat_width), jnp.float32),
            pltpu.VMEM((feat_width, feat_width), jnp.float32),
        ],
        name="whiten",
    )(index, lengths, moments, sums)


def shards(features, seg_lengths):
    frame_rows = features.shape[0]
    feat_width = features.shape[1]
    feat_count = lax.axis_size("feat")
    tm_index = lax.axis_index("tm")
    feat_index = lax.axis_index("feat")
    col_block = feat_width // feat_count
    comp_block = NC // feat_count
    tail_part = from_behind(features[:LAG], "tm", -1)
    ahead_rows = jnp.concatenate([features[LAG:], tail_part], axis=0)
    seg_ends = jnp.cumsum(seg_lengths).astype(jnp.int32)
    moments = tm_index * frame_rows - LAG + jnp.arange(frame_rows + LAG, dtype=jnp.int32)
    inside = (seg_ends[:, None] > moments[None, :]) & (seg_ends[:, None] <= moments[None, :] + LAG)
    clear = jnp.logical_not(jnp.any(inside, axis=0)) & (moments >= 0)
    valid_wide = clear.astype(jnp.float32)
    validity = valid_wide[LAG:]
    uses = (validity + valid_wide[:frame_rows]).astype(jnp.bfloat16)
    start_col = feat_index * col_block
    lead_cols = lax.dynamic_slice_in_dim(features, start_col, col_block, 1)
    gram_rows = contract(lead_cols * uses[:, None], features)
    cross_rows = contract(lead_cols * validity.astype(jnp.bfloat16)[:, None], ahead_rows)
    sums = jnp.dot(uses, features, preferred_element_type=jnp.float32)
    packed = jnp.concatenate(
        [gram_rows, cross_rows, jnp.broadcast_to(sums[None, :], (8, feat_width))], axis=0
    )
    packed = lax.psum(packed, "tm")
    gathered = lax.all_gather(packed[: 2 * col_block], "feat", axis=0, tiled=True)
    koopman_rows, first_part, second_part, offset = whiten(
        feat_index.astype(jnp.int32).reshape(1),
        seg_lengths.reshape(1, -1),
        gathered,
        packed[2 * col_block :],
        col_block,
        comp_block,
    )
    forward = jnp.einsum("cf,tf->ct", first_part, ahead_rows, preferred_element_type=jnp.float32)
    backward = jnp.einsum("cf,tf->ct", second_part, features, preferred_element_type=jnp.float32)
    lag_error = (forward - backward - offset[:, :1]) * validity[None, :]
    return (koopman_rows, lag_error)


def solution(mesh):
    in_specs = (P("tm", None), P())
    out_specs = (P("feat", None), P("feat", "tm"))
    return jax.shard_map(shards, mesh=mesh, in_specs=in_specs, out_specs=out_specs, check_vma=False)
```

profile of v0, /device:TPU:1, one launch (start us, length us, event | category | flops | bytes accessed | tf_op | source)
XLA Modules:
  0.0 327.0 jit_solution(15491687210693857421)
XLA Ops:
  7.2 0.0 all-reduce.2.cloned.1.call-start
  7.2 1.0 slice.24
  8.2 5.1 %collective-permute-start = (bf16[64,512]{1,0:T(8,128)(2,1)S(1)}, bf16[64,512]{1,0:T(8,128)(2,1)S(1)}, u32[]{:S(2)}, u32[]{:S(2)}) collective-permute-start(bf16[64,512]{1,0:T(8,128)(2,1)S(1)} %slice.24), channel_id=1, source_target_pairs={{4,0},{8,4},{12,8},{16,12},{20,16},{24,20},{28,24},{32,28},{36,32}... | collective-permute-start | bytes 196616 | tf_op jit(solution)/shard_map/ppermute | solution.py:19
  13.4 0.8 copy.6
  14.1 0.2 reduce-window.8
  14.3 0.1 reduce
  14.4 1.0 and_reduce_fusion
  15.4 0.1 fusion.16
  15.5 2.7 fusion.4
  18.2 0.4 fusion.17
  18.6 0.1 slice.38
  18.7 0.1 slice.23
  18.9 1.0 fusion.2
  19.8 0.3 copy-done.1
  20.1 0.8 pad_maximum_fusion.3
  21.0 0.0 all-gather.2.cloned.1.call-start
  21.0 180.8 %all-reduce.2.cloned.1.call-done = f32[264,512]{1,0:T(8,128)} async-done(((f32[264,512]{1,0:T(8,128)}), f32[264,512]{1,0:T(8,128)}) %all-reduce.2.cloned.1.call-update) | async-done | bytes 540688 | tf_op jit(solution)/shard_map/psum | solution.py:181
  201.9 1.9 slice.30
  203.8 1.3 slice.31.sums_ref
  205.1 31.7 %all-gather.2.cloned.1.call-done.moments_ref = f32[1024,512]{1,0:T(8,128)} async-done(((f32[256,512]{1,0:T(8,128)}), f32[1024,512]{1,0:T(8,128)}) %all-gather.2.cloned.1.call-update) | async-done | bytes 2097168 | tf_op jit(solution)/shard_map/all_gather | solution.py:182
  236.8 79.4 %whiten.1 = (f32[128,512]{1,0:T(8,128)}, bf16[32,512]{1,0:T(8,128)(2,1)}, bf16[32,512]{1,0:T(8,128)(2,1)}, f32[32,128]{1,0:T(8,128)}) custom-call(s32[1]{0:T(128)} %bitcast.index_ref, s32[1,128]{1,0:T(1,128)} %bitcast.12, f32[1024,512]{1,0:T(8,128)} %all-gather.2.cloned.1.call-done.moments_ref, f32[8,512]{1,0:T(8,128)} %slice.31.sums_ref), custom_call_target="tpu_custom_call" | custom-call | tf_op jit(solution)/shard_map/whiten/pallas_call | solution.py:138
  316.2 1.0 slice_reduce_fusion
  317.2 1.5 fusion.18
  318.7 1.4 fusion.1
  (14 shorter events, 0.1 us)
Async XLA Ops:
  7.2 11.1 %copy-start = (bf16[2048,512]{1,0:T(8,128)(2,1)S(1)}, bf16[2048,512]{1,0:T(8,128)(2,1)}, u32[]{:S(2)}) copy-start(bf16[2048,512]{1,0:T(8,128)(2,1)} %param.2) | copy-start | bytes 6291460
  7.2 194.7 %all-reduce.2.cloned.1.call-start = ((), (), s32[]{:S(2)}) async-start(), calls=%async_computation | async-start | bytes 1081344 | tf_op jit(solution)/shard_map/psum | solution.py:181
  8.2 10.6 %collective-permute-start = (bf16[64,512]{1,0:T(8,128)(2,1)S(1)}, bf16[64,512]{1,0:T(8,128)(2,1)S(1)}, u32[]{:S(2)}, u32[]{:S(2)}) collective-permute-start(bf16[64,512]{1,0:T(8,128)(2,1)S(1)} %slice.24), channel_id=1, source_target_pairs={{4,0},{8,4},{12,8},{16,12},{20,16},{24,20},{28,24},{32,28},{36,32}... | collective-permute-start | bytes 196616 | tf_op jit(solution)/shard_map/ppermute | solution.py:19
  18.8 1.3 copy-start.1
  21.0 215.9 %all-gather.2.cloned.1.call-start = ((), (), s32[]{:S(2)}) async-start(), calls=%async_computation.1 | async-start | bytes 2621440 | tf_op jit(solution)/shard_map/all_gather | solution.py:182
  316.2 2.4 copy-start.2
  316.2 2.5 copy-start.3
Sparse Core Ops, SparseCore 0:
  21.1 180.7 all-reduce.1
  203.9 32.8 all-gather.1
where the time goes:
time: 327 us
  waiting for transfers between devices  213 us (65%)
  Pallas kernels  79.4 us (24%)
  between operations  14.2 us (4%)
  matrix products  6.98 us (2%)
  local copies, waits for them, and re-layouts  6.44 us (2%)
  starting transfers between devices  5.22 us (2%)
    psum x1, waiting for transfers between devices, shards(): packed = lax.psum(packed, 'tm')  181 us
    pallas_call x1, Pallas kernels, whiten(): pl.pallas_call(whiten_kernel, out_shape=(jax.ShapeDtypeStruct((part, feat...  79.4 us
    all_gather x1, waiting for transfers between devices, shards(): lax.all_gather(packed[:2 * col_block], 'feat', axis=0, tiled=True)  31.7 us
  transfers between devices with their start and end apart: 3, of which 2 were waited for; matrix products, arithmetic and copies ran while one was open for 2% of the time, Pallas kernels for 0%

commit v1 on v0

--- a/solution.py
+++ b/solution.py
@@ -11,6 +11,8 @@
 RIDGE = 0.05
 HIGHEST = lax.Precision.HIGHEST
 LEAF = 128
+MESH = pl.DeviceIdType.MESH
+X_CHIPS, Y_CHIPS, Z_CHIPS, CORES = 4, 4, 8, 2
 
 
 def from_behind(shard, axis, by):
@@ -63,38 +65,42 @@
 
 
 def whiten_kernel(
-    index_ref, lengths_ref, moments_ref, sums_ref, koop_ref, first_ref, second_ref, offset_ref, work, cov
+    index_ref, lengths_ref, moments_ref, koop_ref, first_ref, second_ref, offset_ref, work, cov
 ):
     feat_width = work.shape[0]
     blocks = feat_width // LEAF
     part = koop_ref.shape[0]
     pairs = jnp.maximum(lengths_ref[...] - LAG, 0).astype(jnp.float32)
     scale = 1.0 / (2.0 * jnp.sum(pairs, axis=1, keepdims=True))
-    mean = sums_ref[0:1, :] * scale
+
+    def moment(kind, k, m):
+        top, left = LEAF * (2 * k + kind), LEAF * (m % 2)
+        return moments_ref[m // 2, top : top + LEAF, left : left + LEAF]
+
+    def gram_block(k, m):
+        return moment(0, m, k).T if m == (k + blocks - 1) % blocks else moment(0, k, m)
+
+    sums = moment(0, 0, blocks - 1)
+    mean = jnp.concatenate([sums[m : m + 1, :] for m in range(blocks)], axis=1) * scale
     mean_cols = jnp.broadcast_to(mean, (LEAF, feat_width)).T
     rows_io = lax.broadcasted_iota(jnp.int32, (LEAF, LEAF), 0)
     lanes_io = lax.broadcasted_iota(jnp.int32, (LEAF, LEAF), 1)
     eye = rows_io == lanes_io
     trace = jnp.zeros((1, 1), jnp.float32)
     for k in range(blocks):
-        square = moments_ref[2 * LEAF * k : 2 * LEAF * k + LEAF, LEAF * k : LEAF * k + LEAF]
-        square = square * scale - mean_cols[LEAF * k : LEAF * k + LEAF, :] * mean[:, LEAF * k : LEAF * k + LEAF]
+        square = gram_block(k, k) * scale - mean_cols[LEAF * k : LEAF * k + LEAF, :] * mean[:, LEAF * k : LEAF * k + LEAF]
         diag = jnp.sum(jnp.where(eye, square, 0.0), axis=0, keepdims=True)
         trace = trace + jnp.sum(diag, axis=1, keepdims=True)
     ridge = RIDGE * (trace / feat_width)
     for k in range(blocks):
         for m in range(blocks):
             outer = mean_cols[LEAF * k : LEAF * k + LEAF, :] * mean[:, LEAF * m : LEAF * m + LEAF]
-            block = moments_ref[2 * LEAF * k : 2 * LEAF * k + LEAF, LEAF * m : LEAF * m + LEAF] * scale - outer
+            block = gram_block(k, m) * scale - outer
             if k == m:
                 block = block + jnp.where(eye, ridge, 0.0)
             work[LEAF * k : LEAF * k + LEAF, LEAF * m : LEAF * m + LEAF] = block
-            straight = moments_ref[
-                2 * LEAF * k + LEAF : 2 * LEAF * k + 2 * LEAF, LEAF * m : LEAF * m + LEAF
-            ]
-            turned = moments_ref[
-                2 * LEAF * m + LEAF : 2 * LEAF * m + 2 * LEAF, LEAF * k : LEAF * k + LEAF
-            ].T
+            straight = moment(1, k, m)
+            turned = moment(1, m, k).T
             cov[LEAF * k : LEAF * k + LEAF, LEAF * m : LEAF * m + LEAF] = (straight + turned) * scale - outer
 
     def eliminate(k, carry):
@@ -132,8 +138,8 @@
     offset_ref[...] = jnp.broadcast_to(jnp.sum(gap, axis=1, keepdims=True), offset_ref.shape)
 
 
-def whiten(index, lengths, moments, sums, part, comps):
-    feat_width = moments.shape[1]
+def whiten(index, lengths, moments, part, comps):
+    feat_width = 2 * moments.shape[2]
     vmem = pl.BlockSpec(memory_space=pltpu.VMEM)
     return pl.pallas_call(
         whiten_kernel,
@@ -143,14 +149,151 @@
             jax.ShapeDtypeStruct((comps, feat_width), jnp.bfloat16),
             jax.ShapeDtypeStruct((comps, 128), jnp.float32),
         ),
-        in_specs=[pl.BlockSpec(memory_space=pltpu.SMEM), vmem, vmem, vmem],
+        in_specs=[pl.BlockSpec(memory_space=pltpu.SMEM), vmem, vmem],
         out_specs=(vmem, vmem, vmem, vmem),
         scratch_shapes=[
             pltpu.VMEM((feat_width, feat_width), jnp.float32),
             pltpu.VMEM((feat_width, feat_width), jnp.float32),
         ],
         name="whiten",
-    )(index, lengths, moments, sums)
+    )(index, lengths, moments)
+
+
+def total_kernel(
+    mine_ref, out_ref, from_core, held, from_x, from_z, core_send, core_recv, x_send, x_recv, z_send, z_recv,
+    gz_send, gz_recv, ga_send, ga_recv, gb_send, gb_recv, gc_send, gc_recv
+):
+    place, y = lax.axis_index("tm"), lax.axis_index("feat")
+    core = lax.rem(place, CORES)
+    z = lax.rem(lax.div(place, CORES), Z_CHIPS)
+    x = lax.div(place, CORES * Z_CHIPS)
+    rows, half = held.shape
+    x_rows = rows // X_CHIPS
+    z_rows = x_rows // Z_CHIPS
+    split = x_rows // 2
+
+    def at(x_to, z_to, core_to):
+        return {"tm": (x_to * Z_CHIPS + z_to) * CORES + core_to}
+
+    def along_x(step):
+        return at(lax.rem(x + step, X_CHIPS), z, core)
+
+    def along_z(step):
+        return at(x, lax.rem(z + step, Z_CHIPS), core)
+
+    def along_y(step):
+        return {"feat": lax.rem(y + step, Y_CHIPS)}
+
+    partner = at(x, z, 1 - core)
+    peers = [partner]
+    peers += [along_x(step) for step in range(1, X_CHIPS)]
+    peers += [along_z(step) for step in range(1, Z_CHIPS)]
+    peers += [along_y(step) for step in range(1, Y_CHIPS)]
+    barrier = pltpu.get_barrier_semaphore()
+    for peer in peers:
+        pl.semaphore_signal(barrier, inc=1, device_id=peer, device_id_type=MESH)
+    pl.semaphore_wait(barrier, len(peers))
+
+    def send(src, dst, send_sem, recv_sem, peer):
+        copy = pltpu.make_async_remote_copy(
+            src_ref=src, dst_ref=dst, send_sem=send_sem, recv_sem=recv_sem, device_id=peer, device_id_type=MESH
+        )
+        copy.start()
+        return copy
+
+    def finish(copies):
+        for copy in copies:
+            copy.wait()
+
+    other_lanes = pl.ds(pl.multiple_of((1 - core) * half, half), half)
+    own_lanes = pl.ds(pl.multiple_of(core * half, half), half)
+    finish([send(mine_ref.at[:, other_lanes], from_core, core_send, core_recv, partner)])
+    held[...] = mine_ref[:, own_lanes] + from_core[...]
+
+    copies = []
+    for step in range(1, X_CHIPS):
+        to = pl.multiple_of(lax.rem(x + step, X_CHIPS) * x_rows, x_rows)
+        copies.append(
+            send(held.at[pl.ds(to, x_rows), :], from_x.at[step], x_send.at[step], x_recv.at[step], along_x(step))
+        )
+    finish(copies)
+    total = held[pl.ds(pl.multiple_of(x * x_rows, x_rows), x_rows), :]
+    for step in range(1, X_CHIPS):
+        total = total + from_x[step]
+    from_x[0] = total
+
+    copies = []
+    for step in range(1, Z_CHIPS):
+        to = pl.multiple_of(lax.rem(z + step, Z_CHIPS) * z_rows, z_rows)
+        copies.append(
+            send(from_x.at[0, pl.ds(to, z_rows), :], from_z.at[step], z_send.at[step], z_recv.at[step], along_z(step))
+        )
+    finish(copies)
+    own = pl.ds(pl.multiple_of(z * z_rows, z_rows), z_rows)
+    total = from_x[0, own, :]
+    for step in range(1, Z_CHIPS):
+        total = total + from_z[step]
+    out_ref[core, y, x, own, :] = total
+
+    piece = out_ref.at[core, y, x, own, :]
+    finish(
+        [send(piece, piece, gz_send.at[step], gz_recv.at[step], along_z(step)) for step in range(1, Z_CHIPS)]
+    )
+    low, high = pl.ds(0, split), pl.ds(split, split)
+    copies = []
+    piece = out_ref.at[core, y, x, low, :]
+    for step in range(1, X_CHIPS):
+        copies.append(send(piece, piece, ga_send.at[0, step], ga_recv.at[0, step], along_x(step)))
+    piece = out_ref.at[core, y, x, high, :]
+    for step in range(1, Y_CHIPS):
+        copies.append(send(piece, piece, ga_send.at[1, step], ga_recv.at[1, step], along_y(step)))
+    finish(copies)
+    copies = []
+    piece = out_ref.at[core, y, :, low, :]
+    for step in range(1, Y_CHIPS):
+        copies.append(send(piece, piece, gb_send.at[0, step], gb_recv.at[0, step], along_y(step)))
+    piece = out_ref.at[core, :, x, high, :]
+    for step in range(1, X_CHIPS):
+        copies.append(send(piece, piece, gb_send.at[1, step], gb_recv.at[1, step], along_x(step)))
+    finish(copies)
+    piece = out_ref.at[core]
+    finish([send(piece, piece, gc_send, gc_recv, partner)])
+
+
+def total_moments(packed):
+    rows, width = packed.shape
+    half, x_rows = width // CORES, rows // X_CHIPS
+    vmem = pl.BlockSpec(memory_space=pltpu.VMEM)
+    dma = pltpu.SemaphoreType.DMA
+    out = pl.pallas_call(
+        total_kernel,
+        out_shape=jax.ShapeDtypeStruct((CORES, Y_CHIPS, X_CHIPS, x_rows, half), jnp.float32),
+        in_specs=[vmem],
+        out_specs=vmem,
+        scratch_shapes=[
+            pltpu.VMEM((rows, half), jnp.float32),
+            pltpu.VMEM((rows, half), jnp.float32),
+            pltpu.VMEM((X_CHIPS, x_rows, half), jnp.float32),
+            pltpu.VMEM((Z_CHIPS, x_rows // Z_CHIPS, half), jnp.float32),
+            dma,
+            dma,
+            dma((X_CHIPS,)),
+            dma((X_CHIPS,)),
+            dma((Z_CHIPS,)),
+            dma((Z_CHIPS,)),
+            dma((Z_CHIPS,)),
+            dma((Z_CHIPS,)),
+            dma((2, X_CHIPS)),
+            dma((2, X_CHIPS)),
+            dma((2, X_CHIPS)),
+            dma((2, X_CHIPS)),
+            dma,
+            dma,
+        ],
+        compiler_params=pltpu.CompilerParams(collective_id=0, has_side_effects=True),
+        name="total_moments",
+    )(packed)
+    return out.reshape(CORES, Y_CHIPS * rows, half)
 
 
 def shards(features, seg_lengths):
@@ -175,16 +318,14 @@
     gram_rows = contract(lead_cols * uses[:, None], features)
     cross_rows = contract(lead_cols * validity.astype(jnp.bfloat16)[:, None], ahead_rows)
     sums = jnp.dot(uses, features, preferred_element_type=jnp.float32)
-    packed = jnp.concatenate(
-        [gram_rows, cross_rows, jnp.broadcast_to(sums[None, :], (8, feat_width))], axis=0
-    )
-    packed = lax.psum(packed, "tm")
-    gathered = lax.all_gather(packed[: 2 * col_block], "feat", axis=0, tiled=True)
+    sum_rows = jnp.pad(sums.reshape(feat_count, col_block), ((0, 8 - feat_count), (0, 0)))
+    before = lax.rem(feat_index + feat_count - 1, feat_count) * col_block
+    gram_rows = lax.dynamic_update_slice(gram_rows, sum_rows, (0, before))
+    gathered = total_moments(jnp.concatenate([gram_rows, cross_rows], axis=0))
     koopman_rows, first_part, second_part, offset = whiten(
         feat_index.astype(jnp.int32).reshape(1),
         seg_lengths.reshape(1, -1),
         gathered,
-        packed[2 * col_block :],
         col_block,
         comp_block,
     )

time: 327 us -> 142 us (0.43)
  waiting for transfers between devices: 213 us -> 0.01 us
  Pallas kernels: 79.4 us -> 121 us
  between operations: 14.2 us -> 0.74 us
    psum x1 -> x0, waiting for transfers between devices: 181 us -> none  [shards(): packed = lax.psum(packed, 'tm')]
    pallas_call x0 -> x1, Pallas kernels: none -> 41.8 us  [total_moments(): pl.pallas_call(total_kernel, out_shape=jax.ShapeDtypeStruct((CORES, Y_CHI...]
    all_gather x1 -> x0, waiting for transfers between devices: 31.7 us -> none  [shards(): lax.all_gather(packed[:2 * col_block], 'feat', axis=0, tiled=True)]
  transfers between devices with their start and end apart: 3 -> 1, of which waited for: 2 -> 0; matrix products, arithmetic and copies ran while one was open for 2% -> 5% of each run, Pallas kernels for 0% -> 0%
where the time goes in v1:
time: 142 us
  Pallas kernels  121 us (85%)
  matrix products  6.77 us (5%)
  local copies, waits for them, and re-layouts  5.66 us (4%)
  starting transfers between devices  5.14 us (4%)
  other arithmetic  2.15 us (2%)
    pallas_call x1, Pallas kernels, whiten(): pl.pallas_call(whiten_kernel, out_shape=(jax.ShapeDtypeStruct((part, feat...  79.5 us
    pallas_call x1, Pallas kernels, total_moments(): pl.pallas_call(total_kernel, out_shape=jax.ShapeDtypeStruct((CORES, Y_CHI...  41.8 us
    ppermute x1, starting transfers between devices, from_behind(): return lax.ppermute(shard, axis, pairs)  5.14 us
    dot_general x2, matrix products, contract(): lax.dot_general(left_rows, right_rows, (((0,), (0,)), ((), ())), preferre...  3.5 us
    slice x1, local copies, waits for them, and re-layouts, shards(): ahead_rows = jnp.concatenate([features[LAG:], tail_part], axis=0)  2.98 us
  transfers between devices with their start and end apart: 1, of which 0 were waited for; matrix products, arithmetic and copies ran while one was open for 5% of the time, Pallas kernels for 0%

profile of v1, /device:TPU:1, one launch (start us, length us, event | category | flops | bytes accessed | tf_op | source)
XLA Modules:
  0.0 141.8 jit_solution(6751924674142587111)
XLA Ops:
  0.6 0.8 slice.18
  1.5 5.1 %collective-permute-start = (bf16[64,512]{1,0:T(8,128)(2,1)S(1)}, bf16[64,512]{1,0:T(8,128)(2,1)S(1)}, u32[]{:S(2)}, u32[]{:S(2)}) collective-permute-start(bf16[64,512]{1,0:T(8,128)(2,1)S(1)} %slice.18), channel_id=1, source_target_pairs={{4,0},{8,4},{12,8},{16,12},{20,16},{24,20},{28,24},{32,28},{36,32}... | collective-permute-start | bytes 196616 | tf_op jit(solution)/shard_map/ppermute | solution.py:21
  6.6 0.8 copy.6
  7.4 0.2 reduce-window.8
  7.6 0.1 reduce
  7.7 0.0 copy-start
  7.7 1.0 and_reduce_fusion
  8.7 0.1 slice.28
  8.7 0.1 fusion.16
  8.8 3.0 %slice.17 = bf16[1984,512]{1,0:T(8,128)(2,1)} slice(bf16[2048,512]{1,0:T(8,128)(2,1)} %param.2), slice={[64:2048], [0:512]} | slice | bytes 4063232 | tf_op jit(solution)/shard_map/slice | solution.py:308
  11.8 0.0 copy-done
  11.8 0.4 fusion.17
  12.2 1.0 fusion.4
  13.2 0.0 collective-permute-done
  13.2 2.5 %fusion.2 = f32[128,512]{1,0:T(8,128)S(1)} fusion(bf16[64,512]{1,0:T(8,128)(2,1)S(1)} %collective-permute-done, bf16[1984,512]{1,0:T(8,128)(2,1)} %slice.17, bf16[2048,512]{1,0:T(8,128)(2,1)S(1)} %copy-done, s32[]{:T(128)S(6)} %select_n.6, bf16[2048]{0:T(1024)(128)(2,1)S(1)} %slice.28), kind=kOutput, calls=%fused_computation.4 | convolution fusion | flops 273678336 | bytes 2887684 | tf_op jit(solution)/shard_map/dot_general | solution.py:25
  15.7 0.8 pad_maximum_fusion.3.mine_ref
  16.6 41.8 %total_moments.1 = f32[2,4,4,64,256]{4,3,2,1,0:T(8,128)} custom-call(f32[256,512]{1,0:T(8,128)} %pad_maximum_fusion.3.mine_ref), custom_call_target="tpu_custom_call" | custom-call | tf_op jit(solution)/shard_map/total_moments/pallas_call | solution.py:268
  58.4 79.5 %whiten.1 = (f32[128,512]{1,0:T(8,128)}, bf16[32,512]{1,0:T(8,128)(2,1)}, bf16[32,512]{1,0:T(8,128)(2,1)}, f32[32,128]{1,0:T(8,128)}) custom-call(s32[1]{0:T(128)} %bitcast.index_ref, s32[1,128]{1,0:T(1,128)} %bitcast.16, f32[2,1024,256]{2,1,0:T(8,128)} %bitcast.13), custom_call_target="tpu_custom_call" | custom-call | tf_op jit(solution)/shard_map/whiten/pallas_call | solution.py:144
  137.9 0.0 copy-start.1
  137.9 1.0 slice_reduce_fusion
  138.9 1.5 %fusion.18 = f32[32,2048]{1,0:T(8,128)S(1)} fusion(bf16[32,512]{1,0:T(8,128)(2,1)} %get-tuple-element.8, bf16[2048,512]{1,0:T(8,128)(2,1)S(1)} %copy-done), kind=kOutput, calls=%fused_computation.28 | convolution fusion | flops 67108864 | bytes 2392064 | tf_op jit(solution)/shard_map/cf,tf->ct/dot_general | solution.py:333
  140.3 0.0 copy-done.1
  140.4 0.0 copy-done.2
  140.4 1.4 %fusion.1 = f32[32,2048]{1,0:T(8,128)} fusion(f32[32,2048]{1,0:T(8,128)S(1)} %fusion.18, bf16[32,512]{1,0:T(8,128)(2,1)S(1)} %copy-done.2, bf16[64,512]{1,0:T(8,128)(2,1)S(1)} %collective-permute-done, bf16[1984,512]{1,0:T(8,128)(2,1)S(1)} %copy-done.1, f32[2048]{0:T(1024)S(1)} %get-tuple-element.10, f32[32]{0:T(128)S(1)} %slice_reduce_fusion), kind=kOutput, calls=%fused_computation.2 | convolution fusion | flops 71499776 | bytes 2662528 | tf_op jit(solution)/shard_map/cf,tf->ct/dot_general | solution.py:332
  (5 shorter events, 0.0 us)
Async XLA Ops:
  1.5 11.7 %collective-permute-start = (bf16[64,512]{1,0:T(8,128)(2,1)S(1)}, bf16[64,512]{1,0:T(8,128)(2,1)S(1)}, u32[]{:S(2)}, u32[]{:S(2)}) collective-permute-start(bf16[64,512]{1,0:T(8,128)(2,1)S(1)} %slice.18), channel_id=1, source_target_pairs={{4,0},{8,4},{12,8},{16,12},{20,16},{24,20},{28,24},{32,28},{36,32}... | collective-permute-start | bytes 196616 | tf_op jit(solution)/shard_map/ppermute | solution.py:21
  7.7 4.1 %copy-start = (bf16[2048,512]{1,0:T(8,128)(2,1)S(1)}, bf16[2048,512]{1,0:T(8,128)(2,1)}, u32[]{:S(2)}) copy-start(bf16[2048,512]{1,0:T(8,128)(2,1)} %param.2) | copy-start | bytes 6291460
  137.9 2.4 %copy-start.1 = (bf16[1984,512]{1,0:T(8,128)(2,1)S(1)}, bf16[1984,512]{1,0:T(8,128)(2,1)}, u32[]{:S(2)}) copy-start(bf16[1984,512]{1,0:T(8,128)(2,1)} %slice.17) | copy-start | bytes 6094852
  137.9 2.5 %copy-start.2 = (bf16[32,512]{1,0:T(8,128)(2,1)S(1)}, bf16[32,512]{1,0:T(8,128)(2,1)}, u32[]{:S(2)}) copy-start(bf16[32,512]{1,0:T(8,128)(2,1)} %get-tuple-element.7) | copy-start | bytes 98308

commit v2 on v1

--- a/solution.py
+++ b/solution.py
@@ -38,29 +38,54 @@
 
 
 def leaf_inverse(square):
-    tiles = [square[8 * i : 8 * i + 8, :] for i in range(LEAF // 8)]
+    count = LEAF // 8
+    tiles = [square[8 * i : 8 * i + 8, :] for i in range(count)]
     lanes = lax.broadcasted_iota(jnp.int32, (8, LEAF), 1)
     subs = lax.broadcasted_iota(jnp.int32, (8, LEAF), 0)
-    for j in range(LEAF - 1):
-        own, sub = j // 8, j % 8
-        row = jnp.broadcast_to(tiles[own][sub : sub + 1, :], (8, LEAF))
-        pivot = jnp.broadcast_to(row[:, j : j + 1], (8, LEAF))
-        at_pivot = lanes == j
-        row = jnp.where(at_pivot, 1.0, row) / pivot
-        for i in range(own, LEAF // 8):
-            if i == own and sub == 7:
-                continue
-            factor = jnp.broadcast_to(tiles[i][:, j : j + 1], (8, LEAF))
-            updated = jnp.where(at_pivot, 0.0, tiles[i]) - factor * row
-            if i == own:
-                updated = jnp.where(subs > sub, updated, tiles[i])
-            tiles[i] = updated
-    outs = []
-    for i in range(LEAF // 8):
-        rows = subs + 8 * i
-        diag = jnp.sum(jnp.where(lanes == rows, tiles[i], 0.0), axis=1, keepdims=True)
-        unit = jnp.where(lanes < rows, tiles[i], jnp.where(lanes == rows, 1.0, 0.0))
-        outs.append(unit * lax.rsqrt(diag))
+
+    def spread(tile, sub):
+        return jnp.broadcast_to(tile[sub : sub + 1, :], (8, LEAF))
+
+    for g in range(count):
+        first = 8 * g
+        own = tiles[g]
+        columns = [jnp.broadcast_to(own[:, first + k : first + k + 1], (8, LEAF)) for k in range(8)]
+        in_block = (lanes >= first) & (lanes < first + 8)
+        rows = jnp.where(in_block, jnp.where(lanes - first == subs, 1.0, 0.0), own)
+        pivots = columns[0]
+        if g + 1 < count:
+            after = tiles[g + 1]
+            after_columns = [
+                jnp.broadcast_to(after[:, first + k : first + k + 1], (8, LEAF)) for k in range(8)
+            ]
+            after = jnp.where(in_block, 0.0, after)
+        for k in range(8):
+            corner_rows = [spread(columns[m], k) for m in range(k, 8)]
+            row = spread(rows, k)
+            flip = 1.0 / corner_rows[0]
+            pivots = jnp.where(subs == k, columns[k], pivots)
+            factor = jnp.where(subs > k, columns[k] * flip, 0.0)
+            rows = rows - factor * row
+            for m in range(k + 1, 8):
+                columns[m] = columns[m] - factor * corner_rows[m - k]
+            if g + 1 < count:
+                factor = after_columns[k] * flip
+                after = after - factor * row
+                for m in range(k + 1, 8):
+                    after_columns[m] = after_columns[m] - factor * corner_rows[m - k]
+        rows = rows * lax.rsqrt(pivots)
+        tiles[g] = rows
+        if g + 1 < count:
+            tiles[g + 1] = after
+        if g + 2 < count:
+            turned = rows.T
+            spreads = [spread(rows, k) for k in range(8)]
+            for i in range(g + 2, count):
+                tile = jnp.where(in_block, 0.0, tiles[i])
+                for k in range(8):
+                    tile = tile - jnp.broadcast_to(turned[8 * i : 8 * i + 8, k : k + 1], (8, LEAF)) * spreads[k]
+                tiles[i] = tile
+    outs = [jnp.where(lanes <= subs + 8 * i, tiles[i], 0.0) for i in range(count)]
     return jnp.concatenate(outs, axis=0)
 
 
@@ -109,13 +134,15 @@
         work[pl.ds(start, LEAF), pl.ds(start, LEAF)] = jnp.where(eye, 1.0, 0.0)
         panel = exact_dot(inverse, work[pl.ds(start, LEAF), :])
         wide_lanes = lax.broadcasted_iota(jnp.int32, (LEAF, feat_width), 1)
-        below = jnp.where(wide_lanes >= start + LEAF, panel, 0.0)
-        change = exact_dot(below, panel, 0, 0)
         in_block = (wide_lanes >= start) & (wide_lanes < start + LEAF)
-        for i in range(blocks):
-            old = work[LEAF * i : LEAF * i + LEAF, :]
-            old = jnp.where(in_block & (k < i), 0.0, old)
-            work[LEAF * i : LEAF * i + LEAF, :] = old - change[LEAF * i : LEAF * i + LEAF, :]
+        for i in range(1, blocks):
+
+            @pl.when(k < i)
+            def _(i=i):
+                old = jnp.where(in_block, 0.0, work[LEAF * i : LEAF * i + LEAF, :])
+                change = exact_dot(panel[:, LEAF * i : LEAF * i + LEAF], panel, 0, 0)
+                work[LEAF * i : LEAF * i + LEAF, :] = old - change
+
         work[pl.ds(start, LEAF), :] = panel
         return carry
 

time: 142 us -> 91.4 us (0.64)
  Pallas kernels: 121 us -> 70.6 us
    pallas_call x1, Pallas kernels: 79.5 us -> 28.8 us  [whiten(): pl.pallas_call(whiten_kernel, out_shape=(jax.ShapeDtypeStruct((part, feat...]
  transfers between devices with their start and end apart: 1 -> 1, of which waited for: 0 -> 0; matrix products, arithmetic and copies ran while one was open for 5% -> 7% of each run, Pallas kernels for 0% -> 0%
where the time goes in v2:
time: 91.4 us; the launch traced here: 91.1 us
  Pallas kernels  70.6 us (77%)
  matrix products  6.77 us (7%)
  local copies, waits for them, and re-layouts  5.66 us (6%)
  starting transfers between devices  5.14 us (6%)
  other arithmetic  2.15 us (2%)
    pallas_call x1, Pallas kernels, total_moments(): pl.pallas_call(total_kernel, out_shape=jax.ShapeDtypeStruct((CORES, Y_CHI...  41.8 us
    pallas_call x1, Pallas kernels, whiten(): pl.pallas_call(whiten_kernel, out_shape=(jax.ShapeDtypeStruct((part, feat...  28.8 us
    ppermute x1, starting transfers between devices, from_behind(): return lax.ppermute(shard, axis, pairs)  5.14 us
    dot_general x2, matrix products, contract(): lax.dot_general(left_rows, right_rows, (((0,), (0,)), ((), ())), preferre...  3.5 us
    slice x1, local copies, waits for them, and re-layouts, shards(): ahead_rows = jnp.concatenate([features[LAG:], tail_part], axis=0)  2.98 us
  transfers between devices with their start and end apart: 1, of which 0 were waited for; matrix products, arithmetic and copies ran while one was open for 7% of the time, Pallas kernels for 0%

profile of v2, /device:TPU:1, one launch (start us, length us, event | category | flops | bytes accessed | tf_op | source)
XLA Modules:
  0.0 91.1 jit_solution(12589402441971432140)
XLA Ops:
  0.6 0.8 slice.18
  1.5 5.1 %collective-permute-start = (bf16[64,512]{1,0:T(8,128)(2,1)S(1)}, bf16[64,512]{1,0:T(8,128)(2,1)S(1)}, u32[]{:S(2)}, u32[]{:S(2)}) collective-permute-start(bf16[64,512]{1,0:T(8,128)(2,1)S(1)} %slice.18), channel_id=1, source_target_pairs={{4,0},{8,4},{12,8},{16,12},{20,16},{24,20},{28,24},{32,28},{36,32}... | collective-permute-start | bytes 196616 | tf_op jit(solution)/shard_map/ppermute | solution.py:21
  6.6 0.8 copy.6
  7.4 0.2 reduce-window.8
  7.6 0.1 reduce
  7.7 0.0 copy-start
  7.7 1.0 %and_reduce_fusion = pred[2112]{0:T(1024)(128)(4,1)S(1)} fusion(s32[128]{0:T(128)S(1)} %reduce, s32[2112]{0:T(1024)S(1)} %get-tuple-element.13, s32[2112]{0:T(1024)S(1)} %get-tuple-element.12), kind=kLoop, calls=%fused_computation.5 | loop fusion | flops 1079232 | bytes 19520 | tf_op jit(solution)/shard_map/reduce_or | solution.py:339
  8.7 0.1 slice.28
  8.7 0.1 fusion.16
  8.8 3.0 %slice.17 = bf16[1984,512]{1,0:T(8,128)(2,1)} slice(bf16[2048,512]{1,0:T(8,128)(2,1)} %param.2), slice={[64:2048], [0:512]} | slice | bytes 4063232 | tf_op jit(solution)/shard_map/slice | solution.py:335
  11.8 0.0 copy-done
  11.8 0.4 fusion.17
  12.2 1.0 %fusion.4 = f32[128,512]{1,0:T(8,128)S(1)} fusion(bf16[2048,512]{1,0:T(8,128)(2,1)S(1)} %copy-done, s32[]{:T(128)S(6)} %select_n.6, bf16[2048]{0:T(1024)(128)(2,1)S(1)} %get-tuple-element.11), kind=kOutput, calls=%fused_computation.8 | convolution fusion | flops 269484032 | bytes 2887684 | tf_op jit(solution)/shard_map/dot_general | solution.py:25
  13.2 0.0 collective-permute-done
  13.2 2.5 %fusion.2 = f32[128,512]{1,0:T(8,128)S(1)} fusion(bf16[64,512]{1,0:T(8,128)(2,1)S(1)} %collective-permute-done, bf16[1984,512]{1,0:T(8,128)(2,1)} %slice.17, bf16[2048,512]{1,0:T(8,128)(2,1)S(1)} %copy-done, s32[]{:T(128)S(6)} %select_n.6, bf16[2048]{0:T(1024)(128)(2,1)S(1)} %slice.28), kind=kOutput, calls=%fused_computation.4 | convolution fusion | flops 273678336 | bytes 2887684 | tf_op jit(solution)/shard_map/dot_general | solution.py:25
  15.7 0.8 pad_maximum_fusion.3.mine_ref
  16.6 41.8 %total_moments.1 = f32[2,4,4,64,256]{4,3,2,1,0:T(8,128)} custom-call(f32[256,512]{1,0:T(8,128)} %pad_maximum_fusion.3.mine_ref), custom_call_target="tpu_custom_call" | custom-call | tf_op jit(solution)/shard_map/total_moments/pallas_call | solution.py:295
  58.4 28.8 %whiten.1 = (f32[128,512]{1,0:T(8,128)}, bf16[32,512]{1,0:T(8,128)(2,1)}, bf16[32,512]{1,0:T(8,128)(2,1)}, f32[32,128]{1,0:T(8,128)}) custom-call(s32[1]{0:T(128)} %bitcast.index_ref, s32[1,128]{1,0:T(1,128)} %bitcast.16, f32[2,1024,256]{2,1,0:T(8,128)} %bitcast.13), custom_call_target="tpu_custom_call" | custom-call | tf_op jit(solution)/shard_map/whiten/pallas_call | solution.py:171
  87.2 0.0 copy-start.1
  87.2 1.0 %slice_reduce_fusion = f32[32]{0:T(128)S(1)} fusion(f32[32,128]{1,0:T(8,128)} %get-tuple-element.9), kind=kLoop, calls=%fused_computation.14 | loop fusion | bytes 256 | tf_op jit(solution)/shard_map/slice | solution.py:361
  88.2 1.5 %fusion.18 = f32[32,2048]{1,0:T(8,128)S(1)} fusion(bf16[32,512]{1,0:T(8,128)(2,1)} %get-tuple-element.8, bf16[2048,512]{1,0:T(8,128)(2,1)S(1)} %copy-done), kind=kOutput, calls=%fused_computation.28 | convolution fusion | flops 67108864 | bytes 2392064 | tf_op jit(solution)/shard_map/cf,tf->ct/dot_general | solution.py:360
  89.7 0.0 copy-done.1
  89.7 0.0 copy-done.2
  89.7 1.4 %fusion.1 = f32[32,2048]{1,0:T(8,128)} fusion(f32[32,2048]{1,0:T(8,128)S(1)} %fusion.18, bf16[32,512]{1,0:T(8,128)(2,1)S(1)} %copy-done.2, bf16[64,512]{1,0:T(8,128)(2,1)S(1)} %collective-permute-done, bf16[1984,512]{1,0:T(8,128)(2,1)S(1)} %copy-done.1, f32[2048]{0:T(1024)S(1)} %get-tuple-element.10, f32[32]{0:T(128)S(1)} %slice_reduce_fusion), kind=kOutput, calls=%fused_computation.2 | convolution fusion | flops 71499776 | bytes 2662528 | tf_op jit(solution)/shard_map/cf,tf->ct/dot_general | solution.py:359
  (5 shorter events, 0.0 us)
Async XLA Ops:
  1.5 11.7 %collective-permute-start = (bf16[64,512]{1,0:T(8,128)(2,1)S(1)}, bf16[64,512]{1,0:T(8,128)(2,1)S(1)}, u32[]{:S(2)}, u32[]{:S(2)}) collective-permute-start(bf16[64,512]{1,0:T(8,128)(2,1)S(1)} %slice.18), channel_id=1, source_target_pairs={{4,0},{8,4},{12,8},{16,12},{20,16},{24,20},{28,24},{32,28},{36,32}... | collective-permute-start | bytes 196616 | tf_op jit(solution)/shard_map/ppermute | solution.py:21
  7.7 4.1 %copy-start = (bf16[2048,512]{1,0:T(8,128)(2,1)S(1)}, bf16[2048,512]{1,0:T(8,128)(2,1)}, u32[]{:S(2)}) copy-start(bf16[2048,512]{1,0:T(8,128)(2,1)} %param.2) | copy-start | bytes 6291460
  87.2 2.4 %copy-start.1 = (bf16[1984,512]{1,0:T(8,128)(2,1)S(1)}, bf16[1984,512]{1,0:T(8,128)(2,1)}, u32[]{:S(2)}) copy-start(bf16[1984,512]{1,0:T(8,128)(2,1)} %slice.17) | copy-start | bytes 6094852
  87.2 2.5 %copy-start.2 = (bf16[32,512]{1,0:T(8,128)(2,1)S(1)}, bf16[32,512]{1,0:T(8,128)(2,1)}, u32[]{:S(2)}) copy-start(bf16[32,512]{1,0:T(8,128)(2,1)} %get-tuple-element.7) | copy-start | bytes 98308

commit v3 on v2

--- a/solution.py
+++ b/solution.py
@@ -267,24 +267,41 @@
         [send(piece, piece, gz_send.at[step], gz_recv.at[step], along_z(step)) for step in range(1, Z_CHIPS)]
     )
     low, high = pl.ds(0, split), pl.ds(split, split)
-    copies = []
+    forwarded = []
+
+    def forward(piece):
+        slot = len(forwarded)
+        forwarded.append(send(piece, piece, gc_send.at[slot], gc_recv.at[slot], partner))
+
+    def back(place, step, count):
+        return lax.rem(place + count - step, count)
+
+    first_x, first_y, next_x, next_y = [], [], [], []
     piece = out_ref.at[core, y, x, low, :]
     for step in range(1, X_CHIPS):
-        copies.append(send(piece, piece, ga_send.at[0, step], ga_recv.at[0, step], along_x(step)))
+        first_x.append(send(piece, piece, ga_send.at[0, step], ga_recv.at[0, step], along_x(step)))
     piece = out_ref.at[core, y, x, high, :]
     for step in range(1, Y_CHIPS):
-        copies.append(send(piece, piece, ga_send.at[1, step], ga_recv.at[1, step], along_y(step)))
-    finish(copies)
-    copies = []
+        first_y.append(send(piece, piece, ga_send.at[1, step], ga_recv.at[1, step], along_y(step)))
+    forward(out_ref.at[core, y, x])
+    finish(first_x)
     piece = out_ref.at[core, y, :, low, :]
     for step in range(1, Y_CHIPS):
-        copies.append(send(piece, piece, gb_send.at[0, step], gb_recv.at[0, step], along_y(step)))
+        next_y.append(send(piece, piece, gb_send.at[0, step], gb_recv.at[0, step], along_y(step)))
+    finish(first_y)
     piece = out_ref.at[core, :, x, high, :]
     for step in range(1, X_CHIPS):
-        copies.append(send(piece, piece, gb_send.at[1, step], gb_recv.at[1, step], along_x(step)))
-    finish(copies)
-    piece = out_ref.at[core]
-    finish([send(piece, piece, gc_send, gc_recv, partner)])
+        next_x.append(send(piece, piece, gb_send.at[1, step], gb_recv.at[1, step], along_x(step)))
+    for step in range(1, X_CHIPS):
+        forward(out_ref.at[core, y, back(x, step, X_CHIPS), low, :])
+    for step in range(1, Y_CHIPS):
+        forward(out_ref.at[core, back(y, step, Y_CHIPS), x, high, :])
+    for step in (1, 3, 2):
+        next_y[step - 1].wait()
+        forward(out_ref.at[core, back(y, step, Y_CHIPS), :, low, :])
+        next_x[step - 1].wait()
+        forward(out_ref.at[core, :, back(x, step, X_CHIPS), high, :])
+    finish(forwarded)
 
 
 def total_moments(packed):
@@ -314,13 +331,52 @@
             dma((2, X_CHIPS)),
             dma((2, X_CHIPS)),
             dma((2, X_CHIPS)),
-            dma,
-            dma,
+            dma((13,)),
+            dma((13,)),
         ],
         compiler_params=pltpu.CompilerParams(collective_id=0, has_side_effects=True),
         name="total_moments",
     )(packed)
     return out.reshape(CORES, Y_CHIPS * rows, half)
+
+
+def local_kernel(place_ref, ends_ref, features_ref, tail_ref, out_ref):
+    frame_rows, feat_width = features_ref.shape
+    part = out_ref.shape[0] // 2
+    feat = place_ref[1]
+    base = place_ref[0] * frame_rows - LAG
+    ends = ends_ref[...] - base
+    frames = lax.broadcasted_iota(jnp.int32, (frame_rows + LAG, ends.shape[1]), 0)
+    crossed = jnp.where((ends > frames) & (ends <= frames + LAG), 1.0, 0.0)
+    crossed = jnp.max(crossed, axis=1, keepdims=True)
+    index = lax.broadcasted_iota(jnp.int32, (frame_rows + LAG, 1), 0)
+    valid = jnp.where((crossed == 0.0) & (index + base >= 0), 1.0, 0.0)
+    valid = jnp.broadcast_to(valid, (frame_rows + LAG, part))
+    now = valid[LAG:, :].astype(jnp.bfloat16)
+    uses = (valid[LAG:, :] + valid[:frame_rows, :]).astype(jnp.bfloat16)
+    lead = features_ref[:, pl.ds(pl.multiple_of(feat * part, part), part)]
+    kept = lead * now
+    earlier = jnp.concatenate([jnp.zeros((LAG, part), jnp.bfloat16), kept[: frame_rows - LAG, :]], axis=0)
+    left = jnp.concatenate([lead * uses, earlier, uses], axis=1)
+    total = contract(left, features_ref[...])
+    out_ref[:part, :] = total[:part, :]
+    out_ref[part:, :] = total[part : 2 * part, :] + contract(kept[frame_rows - LAG :, :], tail_ref[...])
+    groups = feat_width // part
+    sums = [total[2 * part : 2 * part + 1, part * m : part * m + part] for m in range(groups)]
+    sums.append(jnp.zeros((8 - groups, part), jnp.float32))
+    before = lax.rem(feat + groups - 1, groups) * part
+    out_ref[0:8, pl.ds(pl.multiple_of(before, part), part)] = jnp.concatenate(sums, axis=0)
+
+
+def local_moments(place, ends, features, tail_part, part):
+    vmem = pl.BlockSpec(memory_space=pltpu.VMEM)
+    return pl.pallas_call(
+        local_kernel,
+        out_shape=jax.ShapeDtypeStruct((2 * part, features.shape[1]), jnp.float32),
+        in_specs=[pl.BlockSpec(memory_space=pltpu.SMEM), vmem, vmem, vmem],
+        out_specs=vmem,
+        name="local_moments",
+    )(place, ends, features, tail_part)
 
 
 def shards(features, seg_lengths):
@@ -332,23 +388,13 @@
     col_block = feat_width // feat_count
     comp_block = NC // feat_count
     tail_part = from_behind(features[:LAG], "tm", -1)
-    ahead_rows = jnp.concatenate([features[LAG:], tail_part], axis=0)
     seg_ends = jnp.cumsum(seg_lengths).astype(jnp.int32)
-    moments = tm_index * frame_rows - LAG + jnp.arange(frame_rows + LAG, dtype=jnp.int32)
+    moments = tm_index * frame_rows + jnp.arange(frame_rows, dtype=jnp.int32)
     inside = (seg_ends[:, None] > moments[None, :]) & (seg_ends[:, None] <= moments[None, :] + LAG)
-    clear = jnp.logical_not(jnp.any(inside, axis=0)) & (moments >= 0)
-    valid_wide = clear.astype(jnp.float32)
-    validity = valid_wide[LAG:]
-    uses = (validity + valid_wide[:frame_rows]).astype(jnp.bfloat16)
-    start_col = feat_index * col_block
-    lead_cols = lax.dynamic_slice_in_dim(features, start_col, col_block, 1)
-    gram_rows = contract(lead_cols * uses[:, None], features)
-    cross_rows = contract(lead_cols * validity.astype(jnp.bfloat16)[:, None], ahead_rows)
-    sums = jnp.dot(uses, features, preferred_element_type=jnp.float32)
-    sum_rows = jnp.pad(sums.reshape(feat_count, col_block), ((0, 8 - feat_count), (0, 0)))
-    before = lax.rem(feat_index + feat_count - 1, feat_count) * col_block
-    gram_rows = lax.dynamic_update_slice(gram_rows, sum_rows, (0, before))
-    gathered = total_moments(jnp.concatenate([gram_rows, cross_rows], axis=0))
+    validity = jnp.logical_not(jnp.any(inside, axis=0)).astype(jnp.float32)
+    place = jnp.stack([tm_index, feat_index]).astype(jnp.int32)
+    packed = local_moments(place, seg_ends.reshape(1, -1), features, tail_part, col_block)
+    gathered = total_moments(packed)
     koopman_rows, first_part, second_part, offset = whiten(
         feat_index.astype(jnp.int32).reshape(1),
         seg_lengths.reshape(1, -1),
@@ -356,8 +402,11 @@
         col_block,
         comp_block,
     )
-    forward = jnp.einsum("cf,tf->ct", first_part, ahead_rows, preferred_element_type=jnp.float32)
-    backward = jnp.einsum("cf,tf->ct", second_part, features, preferred_element_type=jnp.float32)
+    maps = jnp.concatenate([first_part, second_part], axis=0)
+    both = jnp.einsum("cf,tf->ct", maps, features, preferred_element_type=jnp.float32)
+    last = jnp.einsum("cf,tf->ct", first_part, tail_part, preferred_element_type=jnp.float32)
+    forward = jnp.concatenate([both[:comp_block, LAG:], last], axis=1)
+    backward = both[comp_block:]
     lag_error = (forward - backward - offset[:, :1]) * validity[None, :]
     return (koopman_rows, lag_error)
 

time: 91.4 us -> 85.9 us (0.940)
  matrix products: 6.77 us -> 1.68 us
  local copies, waits for them, and re-layouts: 5.66 us -> 2.5 us
  Pallas kernels: 70.6 us -> 73 us
    dot_general x5 -> x2, matrix products: 6.77 us -> 1.68 us  [the longest x1 1.56 us: shards(): jnp.einsum('cf,tf->ct', maps, features, preferred_element_type=jnp.float32)]
    pallas_call x0 -> x1, Pallas kernels: none -> 3.79 us  [local_moments(): pl.pallas_call(local_kernel, out_shape=jax.ShapeDtypeStruct((2 * part, fe...]
    slice x2 -> x1, local copies, waits for them, and re-layouts: 3.05 us -> 0.13 us  [shards(): forward = jnp.concatenate([both[:comp_block, LAG:], last], axis=1)]
    pallas_call x1, Pallas kernels: 41.8 us -> 40.4 us  [total_moments(): pl.pallas_call(total_kernel, out_shape=jax.ShapeDtypeStruct((CORES, Y_CHI...]
  transfers between devices with their start and end apart: 1 -> 1, of which waited for: 0 -> 0; matrix products, arithmetic and copies ran while one was open for 7% -> 2% of each run, Pallas kernels for 0% -> 0%
where the time goes in v3:
time: 85.9 us; the launch traced here: 85.1 us
  Pallas kernels  73 us (85%)
  starting transfers between devices  5.14 us (6%)
  local copies, waits for them, and re-layouts  2.5 us (3%)
  other arithmetic  2.04 us (2%)
  matrix products  1.68 us (2%)
    pallas_call x1, Pallas kernels, total_moments(): pl.pallas_call(total_kernel, out_shape=jax.ShapeDtypeStruct((CORES, Y_CHI...  40.4 us
    pallas_call x1, Pallas kernels, whiten(): pl.pallas_call(whiten_kernel, out_shape=(jax.ShapeDtypeStruct((part, feat...  28.8 us
    ppermute x1, starting transfers between devices, from_behind(): return lax.ppermute(shard, axis, pairs)  5.14 us
    pallas_call x1, Pallas kernels, local_moments(): pl.pallas_call(local_kernel, out_shape=jax.ShapeDtypeStruct((2 * part, fe...  3.79 us
  transfers between devices with their start and end apart: 1, of which 0 were waited for; matrix products, arithmetic and copies ran while one was open for 2% of the time, Pallas kernels for 0%

profile of v3, /device:TPU:1, one launch (start us, length us, event | category | flops | bytes accessed | tf_op | source)
XLA Modules:
  0.0 85.1 jit_solution(13878756560504555197)
XLA Ops:
  0.6 0.8 slice.12
  1.5 5.1 %collective-permute-start = (bf16[64,512]{1,0:T(8,128)(2,1)S(1)}, bf16[64,512]{1,0:T(8,128)(2,1)S(1)}, u32[]{:S(2)}, u32[]{:S(2)}) collective-permute-start(bf16[64,512]{1,0:T(8,128)(2,1)S(1)} %slice.12), channel_id=1, source_target_pairs={{4,0},{8,4},{12,8},{16,12},{20,16},{24,20},{28,24},{32,28},{36,32}... | collective-permute-start | bytes 196616 | tf_op jit(solution)/shard_map/ppermute | solution.py:21
  6.6 0.8 copy.6
  7.4 0.2 broadcast_in_dim.4
  7.6 0.1 reduce
  7.7 0.0 copy-start.5
  7.7 0.3 and_reduce_fusion
  8.1 0.6 pad_add_fusion.place_ref
  8.6 0.0 collective-permute-done.tail_ref
  8.6 0.0 copy-start.1
  8.6 0.0 copy-done.5
  8.6 0.6 copy-done.1
  9.3 3.8 %local_moments.1.mine_ref = f32[256,512]{1,0:T(8,128)} custom-call(s32[2]{0:T(128)} %pad_add_fusion.place_ref, s32[1,128]{1,0:T(1,128)} %bitcast.10, bf16[2048,512]{1,0:T(8,128)(2,1)} %features_ref.1, bf16[64,512]{1,0:T(8,128)(2,1)} %copy-done.1), custom_call_target="tpu_custom_call" | custom-call | tf_op jit(solution)/shard_map/local_moments/pallas_call | solution.py:373
  13.1 40.4 %total_moments.1 = f32[2,4,4,64,256]{4,3,2,1,0:T(8,128)} custom-call(f32[256,512]{1,0:T(8,128)} %local_moments.1.mine_ref), custom_call_target="tpu_custom_call" | custom-call | tf_op jit(solution)/shard_map/total_moments/pallas_call | solution.py:312
  53.5 28.8 %whiten.1 = (f32[128,512]{1,0:T(8,128)}, bf16[32,512]{1,0:T(8,128)(2,1)}, bf16[32,512]{1,0:T(8,128)(2,1)}, f32[32,128]{1,0:T(8,128)}) custom-call(s32[1]{0:T(128)} %bitcast.index_ref, s32[1,128]{1,0:T(1,128)} %bitcast.12, f32[2,1024,256]{2,1,0:T(8,128)} %bitcast.9), custom_call_target="tpu_custom_call" | custom-call | tf_op jit(solution)/shard_map/whiten/pallas_call | solution.py:171
  82.3 0.0 copy-done
  82.3 1.6 %fusion.2 = f32[64,2048]{1,0:T(8,128)S(1)} fusion(bf16[2048,512]{1,0:T(8,128)(2,1)S(1)} %copy-done, bf16[32,512]{1,0:T(8,128)(2,1)} %get-tuple-element.8, bf16[32,512]{1,0:T(8,128)(2,1)} %get-tuple-element.7), kind=kOutput, calls=%fused_computation.4 | convolution fusion | flops 134348800 | bytes 2686976 | tf_op jit(solution)/shard_map/cf,tf->ct/dot_general | solution.py:406
  83.9 0.1 slice.16
  84.1 0.0 copy-done.4
  84.1 0.1 slice_reduce_fusion
  84.2 0.0 copy-done.2
  84.2 0.0 copy-done.3
  84.2 0.1 fusion.7
  84.3 0.8 fusion.1
  (6 shorter events, 0.0 us)
Async XLA Ops:
  1.5 7.2 %collective-permute-start = (bf16[64,512]{1,0:T(8,128)(2,1)S(1)}, bf16[64,512]{1,0:T(8,128)(2,1)S(1)}, u32[]{:S(2)}, u32[]{:S(2)}) collective-permute-start(bf16[64,512]{1,0:T(8,128)(2,1)S(1)} %slice.12), channel_id=1, source_target_pairs={{4,0},{8,4},{12,8},{16,12},{20,16},{24,20},{28,24},{32,28},{36,32}... | collective-permute-start | bytes 196616 | tf_op jit(solution)/shard_map/ppermute | solution.py:21
  7.7 1.0 %copy-start.5 = (s32[128]{0:T(128)}, s32[128]{0:T(128)S(1)}, u32[]{:S(2)}) copy-start(s32[128]{0:T(128)S(1)} %reduce) | copy-start | bytes 1540
  8.6 0.6 copy-start.1
  13.1 69.3 %copy-start = (bf16[2048,512]{1,0:T(8,128)(2,1)S(1)}, bf16[2048,512]{1,0:T(8,128)(2,1)}, u32[]{:S(2)}) copy-start(bf16[2048,512]{1,0:T(8,128)(2,1)} %features_ref.1) | copy-start | bytes 6291460
  82.3 1.7 %copy-start.4 = (f32[32,128]{1,0:T(8,128)S(1)}, f32[32,128]{1,0:T(8,128)}, u32[]{:S(2)}) copy-start(f32[32,128]{1,0:T(8,128)} %get-tuple-element.9) | copy-start | bytes 49156
  82.3 1.8 %copy-start.2 = (bf16[64,512]{1,0:T(8,128)(2,1)S(1)}, bf16[64,512]{1,0:T(8,128)(2,1)}, u32[]{:S(2)}) copy-start(bf16[64,512]{1,0:T(8,128)(2,1)} %copy-done.1) | copy-start | bytes 196612
  82.3 1.8 %copy-start.3 = (bf16[32,512]{1,0:T(8,128)(2,1)S(1)}, bf16[32,512]{1,0:T(8,128)(2,1)}, u32[]{:S(2)}) copy-start(bf16[32,512]{1,0:T(8,128)(2,1)} %get-tuple-element.7) | copy-start | bytes 98308

commit v4 on v3

--- a/solution.py
+++ b/solution.py
@@ -11,6 +11,7 @@
 RIDGE = 0.05
 HIGHEST = lax.Precision.HIGHEST
 LEAF = 128
+KERNEL_VMEM = 24 * 1024 * 1024
 MESH = pl.DeviceIdType.MESH
 X_CHIPS, Y_CHIPS, Z_CHIPS, CORES = 4, 4, 8, 2
 
@@ -182,6 +183,7 @@
             pltpu.VMEM((feat_width, feat_width), jnp.float32),
             pltpu.VMEM((feat_width, feat_width), jnp.float32),
         ],
+        compiler_params=pltpu.CompilerParams(vmem_limit_bytes=KERNEL_VMEM),
         name="whiten",
     )(index, lengths, moments)
 
@@ -334,7 +336,9 @@
             dma((13,)),
             dma((13,)),
         ],
-        compiler_params=pltpu.CompilerParams(collective_id=0, has_side_effects=True),
+        compiler_params=pltpu.CompilerParams(
+            collective_id=0, has_side_effects=True, vmem_limit_bytes=KERNEL_VMEM
+        ),
         name="total_moments",
     )(packed)
     return out.reshape(CORES, Y_CHIPS * rows, half)
@@ -375,6 +379,7 @@
         out_shape=jax.ShapeDtypeStruct((2 * part, features.shape[1]), jnp.float32),
         in_specs=[pl.BlockSpec(memory_space=pltpu.SMEM), vmem, vmem, vmem],
         out_specs=vmem,
+        compiler_params=pltpu.CompilerParams(vmem_limit_bytes=KERNEL_VMEM),
         name="local_moments",
     )(place, ends, features, tail_part)
 

time: 85.9 us -> 80.3 us (0.935)
  Pallas kernels: 73 us -> 67.7 us
  local copies, waits for them, and re-layouts: 2.5 us -> 3.45 us
    pallas_call x1, Pallas kernels: 40.4 us -> 38.5 us  [total_moments(): pl.pallas_call(total_kernel, out_shape=jax.ShapeDtypeStruct((CORES, Y_CHI...]
    pallas_call x1, Pallas kernels: 3.79 us -> 1.93 us  [local_moments(): pl.pallas_call(local_kernel, out_shape=jax.ShapeDtypeStruct((2 * part, fe...]
    pallas_call x1, Pallas kernels: 28.8 us -> 27.2 us  [whiten(): pl.pallas_call(whiten_kernel, out_shape=(jax.ShapeDtypeStruct((part, feat...]
    unnamed x12 -> x6, local copies, waits for them, and re-layouts: 0.65 us -> 1.6 us
  transfers between devices with their start and end apart: 1 -> 1, of which waited for: 0 -> 1; matrix products, arithmetic and copies ran while one was open for 2% -> 2% of each run, Pallas kernels for 0% -> 0%
where the time goes in v4:
time: 80.3 us; the launch traced here: 79.6 us
  Pallas kernels  67.7 us (84%)
  starting transfers between devices  5.14 us (6%)
  local copies, waits for them, and re-layouts  3.45 us (4%)
  other arithmetic  1.53 us (2%)
  matrix products  0.87 us (1%)
    pallas_call x1, Pallas kernels, total_moments(): pl.pallas_call(total_kernel, out_shape=jax.ShapeDtypeStruct((CORES, Y_CHI...  38.5 us
    pallas_call x1, Pallas kernels, whiten(): pl.pallas_call(whiten_kernel, out_shape=(jax.ShapeDtypeStruct((part, feat...  27.2 us
    ppermute x1, starting transfers between devices, from_behind(): return lax.ppermute(shard, axis, pairs)  5.14 us
    pallas_call x1, Pallas kernels, local_moments(): pl.pallas_call(local_kernel, out_shape=jax.ShapeDtypeStruct((2 * part, fe...  1.93 us
  transfers between devices with their start and end apart: 1, of which 1 were waited for; matrix products, arithmetic and copies ran while one was open for 2% of the time, Pallas kernels for 0%

profile of v4, /device:TPU:1, one launch (start us, length us, event | category | flops | bytes accessed | tf_op | source)
XLA Modules:
  0.0 79.6 jit_solution(15540894050424879291)
XLA Ops:
  0.6 0.8 %slice.12 = bf16[64,512]{1,0:T(8,128)(2,1)S(1)} slice(bf16[2048,512]{1,0:T(8,128)(2,1)} %features_ref.1), slice={[0:64], [0:512]} | slice | bytes 131072 | tf_op jit(solution)/shard_map/slice | solution.py:395
  1.5 5.1 %collective-permute-start = (bf16[64,512]{1,0:T(8,128)(2,1)S(1)}, bf16[64,512]{1,0:T(8,128)(2,1)S(1)}, u32[]{:S(2)}, u32[]{:S(2)}) collective-permute-start(bf16[64,512]{1,0:T(8,128)(2,1)S(1)} %slice.12), channel_id=1, source_target_pairs={{4,0},{8,4},{12,8},{16,12},{20,16},{24,20},{28,24},{32,28},{36,32}... | collective-permute-start | bytes 196616 | tf_op jit(solution)/shard_map/ppermute | solution.py:22
  6.6 0.8 copy.6
  7.4 0.2 broadcast_in_dim.4
  7.6 0.1 reduce
  7.7 0.3 and_reduce_fusion
  8.0 0.1 pad_add_fusion.place_ref
  8.1 0.2 collective-permute-done.tail_ref
  8.3 0.0 copy-start
  8.3 1.6 %copy-done = bf16[2048,512]{1,0:T(8,128)(2,1)S(1)} copy-done((bf16[2048,512]{1,0:T(8,128)(2,1)S(1)}, bf16[2048,512]{1,0:T(8,128)(2,1)}, u32[]{:S(2)}) %copy-start) | copy-done | bytes 2097176
  9.9 0.0 copy-start.2
  9.9 1.9 %local_moments.1.mine_ref = f32[256,512]{1,0:T(8,128)S(1)} custom-call(s32[2]{0:T(128)S(1)} %pad_add_fusion.place_ref, s32[1,128]{1,0:T(1,128)S(1)} %bitcast.10, bf16[2048,512]{1,0:T(8,128)(2,1)S(1)} %copy-done, bf16[64,512]{1,0:T(8,128)(2,1)S(1)} %collective-permute-done.tail_ref), custom_call_target="tpu_custom_call" | custom-call | tf_op jit(solution)/shard_map/local_moments/pallas_call | solution.py:377
  11.9 0.0 copy-start.1
  11.9 38.5 %total_moments.1 = f32[2,4,4,64,256]{4,3,2,1,0:T(8,128)S(1)} custom-call(f32[256,512]{1,0:T(8,128)S(1)} %local_moments.1.mine_ref), custom_call_target="tpu_custom_call" | custom-call | tf_op jit(solution)/shard_map/total_moments/pallas_call | solution.py:314
  50.4 0.0 copy-done.2
  50.4 27.2 %whiten.1 = (f32[128,512]{1,0:T(8,128)}, bf16[32,512]{1,0:T(8,128)(2,1)S(1)}, bf16[32,512]{1,0:T(8,128)(2,1)S(1)}, f32[32,128]{1,0:T(8,128)S(1)}) custom-call(s32[1]{0:T(128)} %bitcast.index_ref, s32[1,128]{1,0:T(1,128)S(1)} %bitcast.12, f32[2,1024,256]{2,1,0:T(8,128)S(1)} %bitcast.9), custom_call_target="tpu_custom_call" | custom-call | tf_op jit(solution)/shard_map/whiten/pallas_call | solution.py:172
  77.6 0.0 copy-done.1
  77.6 0.7 fusion.2
  78.4 0.1 slice.16
  78.5 0.1 slice_reduce_fusion
  78.6 0.1 fusion.7
  78.8 0.8 %fusion.1 = f32[32,2048]{1,0:T(8,128)} fusion(f32[64,2048]{1,0:T(8,128)S(1)} %fusion.2, f32[32,64]{1,0:T(8,128)S(1)} %fusion.7, f32[32,1984]{1,0:T(8,128)S(1)} %slice.16, f32[2048]{0:T(1024)S(1)} %not_convert_fusion, f32[32]{0:T(128)S(1)} %slice_reduce_fusion), kind=kLoop, calls=%fused_computation.3 | loop fusion | flops 262144 | bytes 794752 | tf_op jit(solution)/shard_map/mul | solution.py:415
  (2 shorter events, 0.0 us)
Async XLA Ops:
  1.5 6.9 %collective-permute-start = (bf16[64,512]{1,0:T(8,128)(2,1)S(1)}, bf16[64,512]{1,0:T(8,128)(2,1)S(1)}, u32[]{:S(2)}, u32[]{:S(2)}) collective-permute-start(bf16[64,512]{1,0:T(8,128)(2,1)S(1)} %slice.12), channel_id=1, source_target_pairs={{4,0},{8,4},{12,8},{16,12},{20,16},{24,20},{28,24},{32,28},{36,32}... | collective-permute-start | bytes 196616 | tf_op jit(solution)/shard_map/ppermute | solution.py:22
  8.3 1.6 %copy-start = (bf16[2048,512]{1,0:T(8,128)(2,1)S(1)}, bf16[2048,512]{1,0:T(8,128)(2,1)}, u32[]{:S(2)}) copy-start(bf16[2048,512]{1,0:T(8,128)(2,1)} %features_ref.1) | copy-start | bytes 6291460
  9.9 40.5 %copy-start.2 = (s32[128]{0:T(128)S(1)}, s32[128]{0:T(128)}, u32[]{:S(2)}) copy-start(s32[128]{0:T(128)} %param.3) | copy-start | bytes 1540
  11.9 65.7 %copy-start.1 = (bf16[2048,512]{1,0:T(8,128)(2,1)S(1)}, bf16[2048,512]{1,0:T(8,128)(2,1)}, u32[]{:S(2)}) copy-start(bf16[2048,512]{1,0:T(8,128)(2,1)} %features_ref.1) | copy-start | bytes 6291460

commit v5 on v4

--- a/solution.py
+++ b/solution.py
@@ -236,15 +236,22 @@
 
     other_lanes = pl.ds(pl.multiple_of((1 - core) * half, half), half)
     own_lanes = pl.ds(pl.multiple_of(core * half, half), half)
-    finish([send(mine_ref.at[:, other_lanes], from_core, core_send, core_recv, partner)])
-    held[...] = mine_ref[:, own_lanes] + from_core[...]
-
+    order = [2, 1, 3, 0]
+    chunks = [pl.ds(pl.multiple_of(lax.rem(x + step, X_CHIPS) * x_rows, x_rows), x_rows) for step in range(X_CHIPS)]
+    swaps = {}
+    for step in order:
+        swaps[step] = send(
+            mine_ref.at[chunks[step], other_lanes], from_core.at[chunks[step], :],
+            core_send.at[step], core_recv.at[step], partner
+        )
     copies = []
-    for step in range(1, X_CHIPS):
-        to = pl.multiple_of(lax.rem(x + step, X_CHIPS) * x_rows, x_rows)
-        copies.append(
-            send(held.at[pl.ds(to, x_rows), :], from_x.at[step], x_send.at[step], x_recv.at[step], along_x(step))
-        )
+    for step in order:
+        swaps[step].wait()
+        held[chunks[step], :] = mine_ref[chunks[step], own_lanes] + from_core[chunks[step], :]
+        if step:
+            copies.append(
+                send(held.at[chunks[step], :], from_x.at[step], x_send.at[step], x_recv.at[step], along_x(step))
+            )
     finish(copies)
     total = held[pl.ds(pl.multiple_of(x * x_rows, x_rows), x_rows), :]
     for step in range(1, X_CHIPS):
@@ -321,8 +328,8 @@
             pltpu.VMEM((rows, half), jnp.float32),
             pltpu.VMEM((X_CHIPS, x_rows, half), jnp.float32),
             pltpu.VMEM((Z_CHIPS, x_rows // Z_CHIPS, half), jnp.float32),
-            dma,
-            dma,
+            dma((X_CHIPS,)),
+            dma((X_CHIPS,)),
             dma((X_CHIPS,)),
             dma((X_CHIPS,)),
             dma((Z_CHIPS,)),

time: 80.3 us -> 80.6 us (level)
    pallas_call x1, Pallas kernels: 38.5 us -> 39.4 us  [total_moments(): pl.pallas_call(total_kernel, out_shape=jax.ShapeDtypeStruct((CORES, Y_CHI...]
where the time goes in v5:
time: 80.6 us; the launch traced here: 80.4 us
  Pallas kernels  68.5 us (85%)
  starting transfers between devices  5.14 us (6%)
  local copies, waits for them, and re-layouts  3.46 us (4%)
  other arithmetic  1.53 us (2%)
  matrix products  0.87 us (1%)
    pallas_call x1, Pallas kernels, total_moments(): pl.pallas_call(total_kernel, out_shape=jax.ShapeDtypeStruct((CORES, Y_CHI...  39.4 us
    pallas_call x1, Pallas kernels, whiten(): pl.pallas_call(whiten_kernel, out_shape=(jax.ShapeDtypeStruct((part, feat...  27.2 us
    ppermute x1, starting transfers between devices, from_behind(): return lax.ppermute(shard, axis, pairs)  5.14 us
    pallas_call x1, Pallas kernels, local_moments(): pl.pallas_call(local_kernel, out_shape=jax.ShapeDtypeStruct((2 * part, fe...  1.93 us
  transfers between devices with their start and end apart: 1, of which 1 were waited for; matrix products, arithmetic and copies ran while one was open for 2% of the time, Pallas kernels for 0%

profile of v5, /device:TPU:1, one launch (start us, length us, event | category | flops | bytes accessed | tf_op | source)
XLA Modules:
  0.0 80.4 jit_solution(7237234614185290518)
XLA Ops:
  0.6 0.8 %slice.12 = bf16[64,512]{1,0:T(8,128)(2,1)S(1)} slice(bf16[2048,512]{1,0:T(8,128)(2,1)} %features_ref.1), slice={[0:64], [0:512]} | slice | bytes 131072 | tf_op jit(solution)/shard_map/slice | solution.py:402
  1.5 5.1 %collective-permute-start = (bf16[64,512]{1,0:T(8,128)(2,1)S(1)}, bf16[64,512]{1,0:T(8,128)(2,1)S(1)}, u32[]{:S(2)}, u32[]{:S(2)}) collective-permute-start(bf16[64,512]{1,0:T(8,128)(2,1)S(1)} %slice.12), channel_id=1, source_target_pairs={{4,0},{8,4},{12,8},{16,12},{20,16},{24,20},{28,24},{32,28},{36,32}... | collective-permute-start | bytes 196616 | tf_op jit(solution)/shard_map/ppermute | solution.py:22
  6.6 0.8 copy.6
  7.4 0.2 broadcast_in_dim.4
  7.6 0.1 reduce
  7.7 0.3 and_reduce_fusion
  8.0 0.1 pad_add_fusion.place_ref
  8.1 0.2 collective-permute-done.tail_ref
  8.3 0.0 copy-start
  8.3 1.6 %copy-done = bf16[2048,512]{1,0:T(8,128)(2,1)S(1)} copy-done((bf16[2048,512]{1,0:T(8,128)(2,1)S(1)}, bf16[2048,512]{1,0:T(8,128)(2,1)}, u32[]{:S(2)}) %copy-start) | copy-done | bytes 2097176
  9.9 0.0 copy-start.2
  9.9 1.9 %local_moments.1.mine_ref = f32[256,512]{1,0:T(8,128)S(1)} custom-call(s32[2]{0:T(128)S(1)} %pad_add_fusion.place_ref, s32[1,128]{1,0:T(1,128)S(1)} %bitcast.10, bf16[2048,512]{1,0:T(8,128)(2,1)S(1)} %copy-done, bf16[64,512]{1,0:T(8,128)(2,1)S(1)} %collective-permute-done.tail_ref), custom_call_target="tpu_custom_call" | custom-call | tf_op jit(solution)/shard_map/local_moments/pallas_call | solution.py:384
  11.9 0.0 copy-start.1
  11.9 39.4 %total_moments.1 = f32[2,4,4,64,256]{4,3,2,1,0:T(8,128)S(1)} custom-call(f32[256,512]{1,0:T(8,128)S(1)} %local_moments.1.mine_ref), custom_call_target="tpu_custom_call" | custom-call | tf_op jit(solution)/shard_map/total_moments/pallas_call | solution.py:321
  51.3 0.0 copy-done.2
  51.3 27.2 %whiten.1 = (f32[128,512]{1,0:T(8,128)}, bf16[32,512]{1,0:T(8,128)(2,1)S(1)}, bf16[32,512]{1,0:T(8,128)(2,1)S(1)}, f32[32,128]{1,0:T(8,128)S(1)}) custom-call(s32[1]{0:T(128)} %bitcast.index_ref, s32[1,128]{1,0:T(1,128)S(1)} %bitcast.12, f32[2,1024,256]{2,1,0:T(8,128)S(1)} %bitcast.9), custom_call_target="tpu_custom_call" | custom-call | tf_op jit(solution)/shard_map/whiten/pallas_call | solution.py:172
  78.5 0.0 copy-done.1
  78.5 0.7 fusion.2
  79.2 0.1 slice.16
  79.4 0.1 slice_reduce_fusion
  79.5 0.1 fusion.7
  79.6 0.8 %fusion.1 = f32[32,2048]{1,0:T(8,128)} fusion(f32[64,2048]{1,0:T(8,128)S(1)} %fusion.2, f32[32,64]{1,0:T(8,128)S(1)} %fusion.7, f32[32,1984]{1,0:T(8,128)S(1)} %slice.16, f32[2048]{0:T(1024)S(1)} %not_convert_fusion, f32[32]{0:T(128)S(1)} %slice_reduce_fusion), kind=kLoop, calls=%fused_computation.3 | loop fusion | flops 262144 | bytes 794752 | tf_op jit(solution)/shard_map/mul | solution.py:422
  (2 shorter events, 0.0 us)
Async XLA Ops:
  1.5 6.9 %collective-permute-start = (bf16[64,512]{1,0:T(8,128)(2,1)S(1)}, bf16[64,512]{1,0:T(8,128)(2,1)S(1)}, u32[]{:S(2)}, u32[]{:S(2)}) collective-permute-start(bf16[64,512]{1,0:T(8,128)(2,1)S(1)} %slice.12), channel_id=1, source_target_pairs={{4,0},{8,4},{12,8},{16,12},{20,16},{24,20},{28,24},{32,28},{36,32}... | collective-permute-start | bytes 196616 | tf_op jit(solution)/shard_map/ppermute | solution.py:22
  8.3 1.6 %copy-start = (bf16[2048,512]{1,0:T(8,128)(2,1)S(1)}, bf16[2048,512]{1,0:T(8,128)(2,1)}, u32[]{:S(2)}) copy-start(bf16[2048,512]{1,0:T(8,128)(2,1)} %features_ref.1) | copy-start | bytes 6291460
  9.9 41.3 %copy-start.2 = (s32[128]{0:T(128)S(1)}, s32[128]{0:T(128)}, u32[]{:S(2)}) copy-start(s32[128]{0:T(128)} %param.3) | copy-start | bytes 1540
  11.9 66.6 %copy-start.1 = (bf16[2048,512]{1,0:T(8,128)(2,1)S(1)}, bf16[2048,512]{1,0:T(8,128)(2,1)}, u32[]{:S(2)}) copy-start(bf16[2048,512]{1,0:T(8,128)(2,1)} %features_ref.1) | copy-start | bytes 6291460
